TPU v7x, 32 devices: a whole 2x2x4 slice. The times are simulated.
32 devices in a mesh: grp: 2 (over y), epoch: 4 (over x, core), asset: 4 (over z).
Axes of the slice: x: 2, y: 2, z: 4, core: 2. Of those that a mesh axis runs over, the one named last changes fastest.
Arguments:
- signals: bfloat16 [8, 1024, 256], P(('grp', 'epoch'), 'asset'), parts along dimension 0, may hold values from -6 to 6
- targets: bfloat16 [8, 1024, 256], P(('grp', 'epoch'), 'asset'), parts along dimension 0, may hold values from -6 to 6
- row_counts: int32 [8, 4], P(('grp', 'epoch'), 'asset'), parts along dimension 0, may hold values from 32 to 256, as said below
- feature_weights: bfloat16 [256, 2048], replicated, may hold values from -0.375 to 0.375
- phases: float32 [2048], replicated, may hold values from -3.140625 to 3.140625
- spread_ids: int32 [2048], replicated, may hold values from 0 to 3
Outputs:
- coefficients: float32 [8, 2048, 256], P(('grp', 'epoch'), 'asset'), parts along dimension 0
There are 2 independent parts, one for each index of `grp`. A program takes and returns all parts, laid end to end along the dimension named above; an argument that names none is the same for every part. Nothing has to cross between parts.
Inputs may be any that keep to these rules, and one draw needn't show every extreme that they name: `row_counts`: each count is at least 32, and in every epoch some asset group has exactly 256 live rows.
All inputs are finite; a program needn't handle non-finite values.
Results may differ from a plain program's by a relative error of at most 0.0003.
Values may be sent and summed in bfloat16 or wider, within the bound.
No kernel may reach another device: no remote copies, remote signals or barrier semaphores. Data moves between devices by JAX's collectives and lax.ppermute only.
A program may use at most 64 MiB of HBM per device.

v0:
```python
import jax
import jax.numpy as jnp
from jax import lax
from jax.sharding import PartitionSpec as P

ITERS = 3
ridge_penalty = 0.05
epsilon = 1e-06


def prefix(part, axis, combine, identity):
    place = lax.axis_index(axis)
    gathered = jax.tree.map(lambda a: lax.all_gather(a, axis), part)
    state = jax.tree.map(lambda a, e: jnp.zeros_like(a) + jnp.asarray(e, a.dtype), part, identity)

    def one(hop, state):
        return combine(
            state, jax.tree.map(lambda a: lax.dynamic_index_in_dim(a, hop, 0, False), gathered)
        )

    return lax.fori_loop(0, place, one, state)


def feature_scale(spread_ids):
    return (
        0.5
        * (
            1.0
            + jnp.where(spread_ids >= 1, 1.0, 0.0)
            + jnp.where(spread_ids >= 2, 2.0, 0.0)
            + jnp.where(spread_ids >= 3, 4.0, 0.0)
        )
    ).astype(jnp.float32)


def make_features(inputs, feature_weights, phases, spread_ids):
    projected = jnp.dot(inputs, feature_weights, preferred_element_type=jnp.float32)
    return jnp.sin(projected * feature_scale(spread_ids) + phases)


def add_pair(earlier, later):
    return (earlier[0] + later[0], earlier[1] + later[1])


def on_device(signals, targets, row_counts, feature_weights, phases, spread_ids):
    rows = signals.shape[1]
    width = feature_weights.shape[1]
    tgt_width = targets.shape[2]
    groups = lax.axis_size("asset")
    block_size = width // groups
    entries = width * tgt_width
    own_rows = row_counts[0, 0]
    all_counts = lax.all_gather(row_counts[0], "asset", axis=0, tiled=True)
    row_sum = jnp.sum(all_counts).astype(jnp.float32)
    inputs = signals[0]
    returns = targets[0]
    features = make_features(inputs, feature_weights, phases, spread_ids)
    live_mask = (jnp.arange(rows) < own_rows)[:, None]
    features = jnp.where(live_mask, features, jnp.zeros_like(features))
    returns = jnp.where(live_mask, returns.astype(jnp.float32), jnp.zeros((), jnp.float32))
    combined = jnp.concatenate([features, returns], axis=1)
    contract_rows = (((0,), (0,)), ((), ()))
    gram_block = lax.psum_scatter(
        lax.dot_general(features, combined, contract_rows, precision=lax.Precision.HIGHEST),
        "asset",
        scatter_dimension=0,
        tiled=True,
    )
    earlier, earlier_rows = prefix(
        (gram_block, row_sum),
        "epoch",
        add_pair,
        (jnp.zeros_like(gram_block), jnp.zeros((), jnp.float32)),
    )
    cumulative = earlier + gram_block
    row_total = earlier_rows + row_sum
    first_row = lax.axis_index("asset") * block_size
    diagonal = jnp.arange(width)[None, :] == first_row + jnp.arange(block_size)[:, None]
    system = cumulative[:, :width] / row_total + ridge_penalty * jnp.where(
        diagonal, 1.0, 0.0
    ).astype(jnp.float32)
    residual = cumulative[:, width:] / row_total
    coef = jnp.zeros((block_size, tgt_width), jnp.float32)
    for iteration in range(ITERS):
        image = jnp.zeros((block_size, tgt_width), jnp.float32) + jnp.dot(
            system,
            lax.all_gather(residual, "asset", axis=0, tiled=True),
            precision=lax.Precision.HIGHEST,
        )
        res_norm, res_curve = lax.psum(
            (jnp.sum(residual * residual), jnp.sum(residual * image)), "asset"
        )
        step_size = res_norm / entries / (res_curve / entries + epsilon)
        coef = coef + step_size * residual
        residual = residual - step_size * image
    return (jnp.sqrt(row_total) * coef)[None]


def solution(mesh):
    placed = (
        P(("grp", "epoch"), "asset", None),
        P(("grp", "epoch"), "asset", None),
        P(("grp", "epoch"), "asset"),
        P(),
        P(),
        P(),
    )
    return jax.shard_map(
        on_device,
        mesh=mesh,
        in_specs=placed,
        out_specs=P(("grp", "epoch"), "asset", None),
        check_vma=False,
    )
```

profile of v0, /device:TPU:0, one launch (start us, length us, event | category | flops | bytes accessed | tf_op | source)
XLA Modules:
  0.0 710.5 jit_solution(8003672284095175270)
XLA Ops:
  8.0 1.0 convert_select_fusion
  9.0 8.1 %fusion.3 = f32[256,2048]{1,0:T(8,128)S(1)} fusion(bf16[256,2048]{1,0:T(8,128)(2,1)S(1)} %copy-done, f32[2048]{0:T(1024)} %param.12, f32[2048]{0:T(1024)S(1)} %add_multiply_fusion, pred[256]{0:T(512)(128)(4,1)S(1)} %iota_compare_fusion.1, bf16[1,256,256]{2,1,0:T(8,128)(2,1)} %param.8), kind=kOutput, calls=%fused_computation.7 | convolution fusion | flops 270008320 | bytes 3293440 | tf_op jit(solution)/shard_map/dot_general | solution.py:37
  17.1 19.4 %fusion.4 = f32[2048,2304]{1,0:T(8,128)} fusion(f32[256,2048]{1,0:T(8,128)S(1)} %fusion.3, f32[256,256]{1,0:T(8,128)S(1)} %convert_select_fusion), kind=kOutput, calls=%fused_computation.8 | convolution fusion | flops 14496104448 | bytes 21233664 | tf_op jit(solution)/shard_map/dot_general | solution.py:64
  36.6 316.7 %reduce-scatter.2.cloned.1.call-done = f32[512,2304]{1,0:T(8,128)} async-done(((f32[2048,2304]{1,0:T(8,128)}), f32[512,2304]{1,0:T(8,128)}) %reduce-scatter.2.cloned.1.call-update) | async-done | bytes 4718608 | tf_op jit(solution)/shard_map/reduce_scatter | solution.py:63
  354.6 9.3 %all-reduce = s32[4]{0:T(128)S(1)} all-reduce(s32[4]{0:T(128)S(1)} %bitcast_dynamic-update-slice_fusion), channel_id=3, replica_groups=mesh['grp'=2,'epoch'=4,'asset'=4] {'asset'}, use_global_device_ids=true, to_apply=%add | all-reduce | flops 4 | bytes 32
  366.6 5.6 all-reduce.1
  372.2 103.7 %all-gather.13.cloned.1.call-done = f32[2048,2304]{1,0:T(8,128)} async-done(((f32[512,2304]{1,0:T(8,128)}), f32[2048,2304]{1,0:T(8,128)}) %all-gather.13.cloned.1.call-update) | async-done | bytes 18874384 | tf_op jit(solution)/shard_map/all_gather | solution.py:13
  475.9 2.5 broadcast_in_dim.58
  478.4 4.3 add.88
  482.8 2.1 copy-done.2
  484.9 0.8 slice_divide_fusion.1
  485.8 5.1 fusion
  490.9 64.1 %all-gather.7.cloned.1.call-done = f32[2048,256]{1,0:T(8,128)} async-done(((f32[512,256]{1,0:T(8,128)}), f32[2048,256]{1,0:T(8,128)}) %all-gather.7.cloned.1.call-update) | async-done | bytes 2097168 | tf_op jit(solution)/shard_map/all_gather | solution.py:87
  555.1 6.6 multiply_reduce_fusion.3
  561.7 10.4 %all-reduce.4 = (f32[]{:T(128)}, f32[]{:T(128)}) all-reduce(f32[]{:T(128)} %get-tuple-element.44, f32[]{:T(128)} %get-tuple-element.43), channel_id=1, replica_groups=mesh['grp'=2,'epoch'=4,'asset'=4] {'asset'}, use_global_device_ids=true, to_apply=%region_5.6 | all-reduce | flops 2 | bytes 16 | tf_op jit(solution)/shard_map/psum | solution.py:90
  573.4 1.9 multiply_subtract_fusion.1
  575.6 43.8 %all-gather.9.cloned.1.call-done = f32[2048,256]{1,0:T(8,128)} async-done(((f32[512,256]{1,0:T(8,128)}), f32[2048,256]{1,0:T(8,128)}) %all-gather.9.cloned.1.call-update) | async-done | bytes 2097168 | tf_op jit(solution)/shard_map/all_gather | solution.py:87
  619.4 6.9 multiply_reduce_fusion.1
  626.3 10.4 %all-reduce.3 = (f32[]{:T(128)}, f32[]{:T(128)}) all-reduce(f32[]{:T(128)} %get-tuple-element.42, f32[]{:T(128)} %get-tuple-element.41), channel_id=1, replica_groups=mesh['grp'=2,'epoch'=4,'asset'=4] {'asset'}, use_global_device_ids=true, to_apply=%region_9.10 | all-reduce | flops 2 | bytes 16 | tf_op jit(solution)/shard_map/psum | solution.py:90
  638.0 1.4 multiply_reduce_fusion
  639.5 44.0 %all-gather.11.cloned.1.call-done = f32[2048,256]{1,0:T(8,128)} async-done(((f32[512,256]{1,0:T(8,128)}), f32[2048,256]{1,0:T(8,128)}) %all-gather.11.cloned.1.call-update) | async-done | bytes 2097168 | tf_op jit(solution)/shard_map/all_gather | solution.py:87
  683.5 6.9 fusion.8
  690.4 10.4 %all-reduce.2 = (f32[]{:T(128)}, f32[]{:T(128)}) all-reduce(f32[]{:T(128)} %get-tuple-element.63, f32[]{:T(128)} %fusion.8), channel_id=1, replica_groups=mesh['grp'=2,'epoch'=4,'asset'=4] {'asset'}, use_global_device_ids=true, to_apply=%region_13.14 | all-reduce | flops 2 | bytes 16 | tf_op jit(solution)/shard_map/psum | solution.py:90
  702.0 2.0 multiply_bitcast_fusion
  (36 shorter events, 4.4 us)
Async XLA Ops:
  6.5 2.5 copy-start
  6.5 346.8 %reduce-scatter.2.cloned.1.call-start = ((), (), s32[]{:S(2)}) async-start(), calls=%async_computation.1 | async-start | bytes 23592960 | tf_op jit(solution)/shard_map/reduce_scatter | solution.py:63
  36.5 316.9 %copy-start.7 = (u32[32]{0:T(128)S(1)}, u32[32]{0:T(128)}, u32[]{:S(2)}) copy-start(u32[32]{0:T(128)} %constant.59) | copy-start | bytes 388
  36.6 328.6 %copy-start.6 = (u32[32]{0:T(128)S(1)}, u32[32]{0:T(128)}, u32[]{:S(2)}) copy-start(u32[32]{0:T(128)} %constant.64) | copy-start | bytes 388
  36.6 439.3 %all-gather.13.cloned.1.call-start = ((), (), s32[]{:S(2)}) async-start(), calls=%async_computation.5 | async-start | bytes 23592960 | tf_op jit(solution)/shard_map/all_gather | solution.py:13
  353.4 201.7 %all-gather.7.cloned.1.call-start = ((), (), s32[]{:S(2)}) async-start(), calls=%async_computation.2 | async-start | bytes 2621440 | tf_op jit(solution)/shard_map/all_gather | solution.py:87
  482.8 2.1 copy-start.2
  485.7 133.6 %all-gather.9.cloned.1.call-start = ((), (), s32[]{:S(2)}) async-start(), calls=%async_computation.3 | async-start | bytes 2621440 | tf_op jit(solution)/shard_map/all_gather | solution.py:87
  485.8 69.3 %copy-start.5 = (f32[512,256]{1,0:T(8,128)S(1)}, f32[512,256]{1,0:T(8,128)}, u32[]{:S(2)}) copy-start(f32[512,256]{1,0:T(8,128)} %slice_divide_fusion.1) | copy-start | bytes 1572868
  575.3 62.7 %copy-start.3 = (f32[512,256]{1,0:T(8,128)S(1)}, f32[512,256]{1,0:T(8,128)}, u32[]{:S(2)}) copy-start(f32[512,256]{1,0:T(8,128)} %multiply_subtract_fusion.1) | copy-start | bytes 1572868
  575.3 108.2 %all-gather.11.cloned.1.call-start = ((), (), s32[]{:S(2)}) async-start(), calls=%async_computation.4 | async-start | bytes 2621440 | tf_op jit(solution)/shard_map/all_gather | solution.py:87
  639.4 62.6 %copy-start.4 = (f32[512,256]{1,0:T(8,128)S(1)}, f32[512,256]{1,0:T(8,128)}, u32[]{:S(2)}) copy-start(f32[512,256]{1,0:T(8,128)} %get-tuple-element.64) | copy-start | bytes 1572868
  639.5 64.5 %copy-start.1 = (bf16[256,2048]{1,0:T(8,128)(2,1)S(1)}, bf16[256,2048]{1,0:T(8,128)(2,1)}, u32[]{:S(2)}) copy-start(bf16[256,2048]{1,0:T(8,128)(2,1)} %param.11) | copy-start | bytes 3145732
Sparse Core Ops, SparseCore 0:
  36.7 316.6 reduce-scatter.1
  354.9 120.9 all-gather.12
  485.9 69.1 all-gather.6
  575.5 43.8 all-gather.8
  639.6 43.8 all-gather.10
where the time goes:
time: 711 us
  waiting for transfers between devices  572 us (80%)
  matrix products  48 us (7%)
  blocking collectives  46.1 us (6%)
  between operations  18.6 us (3%)
  other arithmetic  17.9 us (3%)
  local copies, waits for them, and re-layouts  7.23 us (1%)
    reduce_scatter x1, waiting for transfers between devices, on_device(): lax.psum_scatter(lax.dot_general(features, combined, contract_rows, preci...  317 us
    all_gather x3, waiting for transfers between devices, on_device(): lax.all_gather(residual, 'asset', axis=0, tiled=True)  152 us
    all_gather x1, waiting for transfers between devices, prefix(): gathered = jax.tree.map(lambda a: lax.all_gather(a, axis), part)  104 us
    psum x3, blocking collectives, on_device(): lax.psum((jnp.sum(residual * residual), jnp.sum(residual * image)), 'asset')  31.1 us
    dot_general x3, matrix products, on_device(): jnp.dot(system, lax.all_gather(residual, 'asset', axis=0, tiled=True), pr...  20.5 us
    dot_general x1, matrix products, on_device(): lax.dot_general(features, combined, contract_rows, precision=lax.Precisio...  19.4 us
    unnamed x2, blocking collectives  14.9 us
  transfers between devices with their start and end apart: 5, of which 5 were waited for; matrix products, arithmetic and copies ran while one was open for 1% of the time, Pallas kernels for 0%

commit v1 on v0

--- a/solution.py
+++ b/solution.py
@@ -6,6 +6,19 @@
 ITERS = 3
 ridge_penalty = 0.05
 epsilon = 1e-06
+
+
+def gather_around(x, axis, dim):
+    ways = lax.axis_size(axis)
+    up = [(d, (d + 1) % ways) for d in range(ways)]
+    down = [(d, (d - 1) % ways) for d in range(ways)]
+    earlier, later = ([x], [x])
+    for _ in range(ways // 2):
+        earlier.append(lax.ppermute(earlier[-1], axis, up))
+    for _ in range((ways - 1) // 2):
+        later.append(lax.ppermute(later[-1], axis, down))
+    line = jnp.concatenate([*earlier[::-1], *later[1:]], axis=dim)
+    return jnp.roll(line, (lax.axis_index(axis) - ways // 2) * x.shape[dim], axis=dim)
 
 
 def prefix(part, axis, combine, identity):
@@ -83,9 +96,7 @@
     coef = jnp.zeros((block_size, tgt_width), jnp.float32)
     for iteration in range(ITERS):
         image = jnp.zeros((block_size, tgt_width), jnp.float32) + jnp.dot(
-            system,
-            lax.all_gather(residual, "asset", axis=0, tiled=True),
-            precision=lax.Precision.HIGHEST,
+            system, gather_around(residual, "asset", 0), precision=lax.Precision.HIGHEST
         )
         res_norm, res_curve = lax.psum(
             (jnp.sum(residual * residual), jnp.sum(residual * image)), "asset"

time: 711 us -> 675 us (0.949)
  the two profiles are of different devices: /device:TPU:0 before, /device:TPU:2 now
where the time goes in v1:
time: 675 us
  waiting for transfers between devices  512 us (76%)
  matrix products  52.5 us (8%)
  blocking collectives  46.1 us (7%)
  other arithmetic  23.7 us (4%)
  between operations  18.8 us (3%)
  starting transfers between devices  11.6 us (2%)
  local copies, waits for them, and re-layouts  8.43 us (1%)
    reduce_scatter x1, waiting for transfers between devices, on_device(): lax.psum_scatter(lax.dot_general(features, combined, contract_rows, preci...  315 us
    all_gather x1, waiting for transfers between devices, prefix(): gathered = jax.tree.map(lambda a: lax.all_gather(a, axis), part)  102 us
    ppermute x6, waiting for transfers between devices, gather_around(): earlier.append(lax.ppermute(earlier[-1], axis, up))  50.1 us
    ppermute x3, waiting for transfers between devices, gather_around(): later.append(lax.ppermute(later[-1], axis, down))  44.6 us
    psum x3, blocking collectives, on_device(): lax.psum((jnp.sum(residual * residual), jnp.sum(residual * image)), 'asset')  30.9 us
    dot_general x3, matrix products, on_device(): jnp.dot(system, gather_around(residual, 'asset', 0), precision=lax.Precis...  25 us
    dot_general x1, matrix products, on_device(): lax.dot_general(features, combined, contract_rows, precision=lax.Precisio...  19.4 us
    unnamed x2, blocking collectives  15.2 us
  transfers between devices with their start and end apart: 11, of which 11 were waited for; matrix products, arithmetic and copies ran while one was open for 0% of the time, Pallas kernels for 0%

profile of v1, /device:TPU:2, one launch (start us, length us, event | category | flops | bytes accessed | tf_op | source)
XLA Modules:
  0.0 674.9 jit_solution(16456075464958745450)
XLA Ops:
  9.0 8.1 %fusion.3 = f32[256,2048]{1,0:T(8,128)S(1)} fusion(bf16[256,2048]{1,0:T(8,128)(2,1)S(1)} %copy-done, f32[2048]{0:T(1024)} %param.14, f32[2048]{0:T(1024)S(1)} %add_multiply_fusion, pred[256]{0:T(512)(128)(4,1)S(1)} %iota_compare_fusion.1, bf16[1,256,256]{2,1,0:T(8,128)(2,1)} %param.10), kind=kOutput, calls=%fused_computation.31 | convolution fusion | flops 270008320 | bytes 3293440 | tf_op jit(solution)/shard_map/dot_general | solution.py:50
  17.1 19.4 %fusion.4 = f32[2048,2304]{1,0:T(8,128)} fusion(f32[256,2048]{1,0:T(8,128)S(1)} %fusion.3, f32[256,256]{1,0:T(8,128)S(1)} %convert_select_fusion), kind=kOutput, calls=%fused_computation.32 | convolution fusion | flops 14496104448 | bytes 21233664 | tf_op jit(solution)/shard_map/dot_general | solution.py:77
  36.6 315.2 %reduce-scatter.2.cloned.1.call-done = f32[512,2304]{1,0:T(8,128)} async-done(((f32[2048,2304]{1,0:T(8,128)}), f32[512,2304]{1,0:T(8,128)}) %reduce-scatter.2.cloned.1.call-update) | async-done | bytes 4718608 | tf_op jit(solution)/shard_map/reduce_scatter | solution.py:76
  353.1 9.3 %all-reduce = s32[4]{0:T(128)S(1)} all-reduce(s32[4]{0:T(128)S(1)} %bitcast_dynamic-update-slice_fusion), channel_id=3, replica_groups=mesh['grp'=2,'epoch'=4,'asset'=4] {'asset'}, use_global_device_ids=true, to_apply=%add | all-reduce | flops 4 | bytes 32
  365.0 5.9 all-reduce.1
  370.9 102.4 %all-gather.4.cloned.1.call-done = f32[2048,2304]{1,0:T(8,128)} async-done(((f32[512,2304]{1,0:T(8,128)}), f32[2048,2304]{1,0:T(8,128)}) %all-gather.4.cloned.1.call-update) | async-done | bytes 18874384 | tf_op jit(solution)/shard_map/all_gather | solution.py:26
  475.9 15.6 %while.12 = (s32[]{:T(128)}, f32[512,2304]{1,0:T(8,128)}, f32[]{:T(128)}, s32[]{:T(128)}, f32[4,512,2304]{2,1,0:T(8,128)}, /*index=5*/f32[4]{0:T(128)S(1)}, s32[]{:T(128)}, s32[]{:T(128)}, s32[]{:T(128)}) while((s32[]{:T(128)}, f32[512,2304]{1,0:T(8,128)}, f32[]{:T(128)}, s32[]{:T(128)}, f32[4,512,2304]{2,1,0:T(8,128)}, ...), condition=%wide.region_3.4_spmd, body=%wide.region_2.3_spmd.sunk | while | flops 1179654 | bytes 14155939 | solution.py:34
  475.9 6.6 bitcast_add_fusion.2
  483.7 6.6 bitcast_add_fusion.2
  491.5 4.3 add.97
  501.9 7.3 %collective-permute-done = f32[512,256]{1,0:T(8,128)S(1)} collective-permute-done((f32[512,256]{1,0:T(8,128)S(1)}, f32[512,256]{1,0:T(8,128)S(1)}, u32[]{:S(2)}, u32[]{:S(2)}) %collective-permute-start) | collective-permute-done | bytes 524320 | tf_op jit(solution)/shard_map/ppermute | solution.py:17
  509.2 21.0 %collective-permute-done.2 = f32[512,256]{1,0:T(8,128)S(1)} collective-permute-done((f32[512,256]{1,0:T(8,128)S(1)}, f32[512,256]{1,0:T(8,128)S(1)}, u32[]{:S(2)}, u32[]{:S(2)}) %collective-permute-start.2) | collective-permute-done | bytes 524320 | tf_op jit(solution)/shard_map/ppermute | solution.py:19
  530.3 8.4 %multiply_reduce_fusion.3 = (f32[]{:T(128)}, f32[]{:T(128)}, f32[512,256]{1,0:T(8,128)S(1)}) fusion(f32[512,256]{1,0:T(8,128)S(1)} %slice_divide_fusion.1, s32[]{:T(128)S(6)} %select_n.49, f32[512,256]{1,0:T(8,128)} %collective-permute-done.1, f32[512,256]{1,0:T(8,128)S(1)} %collective-permute-done, f32[512,256]{1,0:T(8,128)S(1)} %collective-permute-done.2, ...), kind=kOutput, calls=%fused_computation.69 | convolution fusion | flops 3230662656 | bytes 7342096 | tf_op jit(solution)/shard_map/dot_general | solution.py:98
  538.6 10.5 %all-reduce.4 = (f32[]{:T(128)}, f32[]{:T(128)}) all-reduce(f32[]{:T(128)} %get-tuple-element.45, f32[]{:T(128)} %get-tuple-element.44), channel_id=1, replica_groups=mesh['grp'=2,'epoch'=4,'asset'=4] {'asset'}, use_global_device_ids=true, to_apply=%region_5.6 | all-reduce | flops 2 | bytes 16 | tf_op jit(solution)/shard_map/psum | solution.py:101
  555.4 9.0 %collective-permute-done.3 = f32[512,256]{1,0:T(8,128)S(1)} collective-permute-done((f32[512,256]{1,0:T(8,128)S(1)}, f32[512,256]{1,0:T(8,128)S(1)}, u32[]{:S(2)}, u32[]{:S(2)}) %collective-permute-start.3) | collective-permute-done | bytes 524320 | tf_op jit(solution)/shard_map/ppermute | solution.py:17
  564.4 13.1 %collective-permute-done.5 = f32[512,256]{1,0:T(8,128)S(1)} collective-permute-done((f32[512,256]{1,0:T(8,128)S(1)}, f32[512,256]{1,0:T(8,128)S(1)}, u32[]{:S(2)}, u32[]{:S(2)}) %collective-permute-start.5) | collective-permute-done | bytes 524320 | tf_op jit(solution)/shard_map/ppermute | solution.py:19
  577.5 9.3 %collective-permute-done.4 = f32[512,256]{1,0:T(8,128)S(1)} collective-permute-done((f32[512,256]{1,0:T(8,128)S(1)}, f32[512,256]{1,0:T(8,128)S(1)}, u32[]{:S(2)}, u32[]{:S(2)}) %collective-permute-start.4) | collective-permute-done | bytes 524320 | tf_op jit(solution)/shard_map/ppermute | solution.py:17
  586.8 8.3 %multiply_reduce_fusion.1 = (f32[]{:T(128)}, f32[]{:T(128)}, f32[512,256]{1,0:T(8,128)S(1)}) fusion(f32[512,256]{1,0:T(8,128)S(1)} %multiply_subtract_fusion.1, s32[]{:T(128)S(6)} %select_n.49, f32[512,256]{1,0:T(8,128)S(1)} %collective-permute-done.4, f32[512,256]{1,0:T(8,128)S(1)} %collective-permute-done.3, f32[512,256]{1,0:T(8,128)S(1)} %collective-permute-done.5, ...), kind=kOutput, calls=%fused_computation.66 | convolution fusion | flops 3230662656 | bytes 7342096 | tf_op jit(solution)/shard_map/dot_general | solution.py:98
  595.2 9.7 %all-reduce.3 = (f32[]{:T(128)}, f32[]{:T(128)}) all-reduce(f32[]{:T(128)} %get-tuple-element.43, f32[]{:T(128)} %get-tuple-element.42), channel_id=1, replica_groups=mesh['grp'=2,'epoch'=4,'asset'=4] {'asset'}, use_global_device_ids=true, to_apply=%region_9.11 | all-reduce | flops 2 | bytes 16 | tf_op jit(solution)/shard_map/psum | solution.py:101
  610.7 12.5 %collective-permute-done.6 = f32[512,256]{1,0:T(8,128)S(1)} collective-permute-done((f32[512,256]{1,0:T(8,128)S(1)}, f32[512,256]{1,0:T(8,128)S(1)}, u32[]{:S(2)}, u32[]{:S(2)}) %collective-permute-start.6) | collective-permute-done | bytes 524320 | tf_op jit(solution)/shard_map/ppermute | solution.py:17
  623.3 10.5 %collective-permute-done.8 = f32[512,256]{1,0:T(8,128)S(1)} collective-permute-done((f32[512,256]{1,0:T(8,128)S(1)}, f32[512,256]{1,0:T(8,128)S(1)}, u32[]{:S(2)}, u32[]{:S(2)}) %collective-permute-start.8) | collective-permute-done | bytes 524320 | tf_op jit(solution)/shard_map/ppermute | solution.py:19
  633.8 11.9 %collective-permute-done.7 = f32[512,256]{1,0:T(8,128)} collective-permute-done((f32[512,256]{1,0:T(8,128)S(1)}, f32[512,256]{1,0:T(8,128)}, u32[]{:S(2)}, u32[]{:S(2)}) %collective-permute-start.7) | collective-permute-done | bytes 524320 | tf_op jit(solution)/shard_map/ppermute | solution.py:17
  645.7 8.3 %fusion.41 = f32[]{:T(128)} fusion(f32[512,256]{1,0:T(8,128)S(1)} %get-tuple-element.65, s32[]{:T(128)S(6)} %select_n.49, f32[512,256]{1,0:T(8,128)} %collective-permute-done.7, f32[512,256]{1,0:T(8,128)S(1)} %collective-permute-done.6, f32[512,256]{1,0:T(8,128)S(1)} %collective-permute-done.8, f32[512,2304]{1,0:T(8,128)} %copy-done.1, ...), kind=kOutput, calls=%fused_computation.61 | convolution fusion | flops 3230400512 | bytes 6817804 | tf_op jit(solution)/shard_map/dot_general | solution.py:98
  654.1 10.7 %all-reduce.2 = (f32[]{:T(128)}, f32[]{:T(128)}) all-reduce(f32[]{:T(128)} %get-tuple-element.64, f32[]{:T(128)} %fusion.41), channel_id=1, replica_groups=mesh['grp'=2,'epoch'=4,'asset'=4] {'asset'}, use_global_device_ids=true, to_apply=%region_13.15 | all-reduce | flops 2 | bytes 16 | tf_op jit(solution)/shard_map/psum | solution.py:101
  (40 shorter events, 26.5 us)
Async XLA Ops:
  6.5 2.5 copy-start
  6.5 345.3 %reduce-scatter.2.cloned.1.call-start = ((), (), s32[]{:S(2)}) async-start(), calls=%async_computation.1 | async-start | bytes 23592960 | tf_op jit(solution)/shard_map/reduce_scatter | solution.py:76
  36.5 315.3 %copy-start.3 = (u32[32]{0:T(128)S(1)}, u32[32]{0:T(128)}, u32[]{:S(2)}) copy-start(u32[32]{0:T(128)} %constant.79) | copy-start | bytes 388
  36.6 327.1 %copy-start.2 = (u32[32]{0:T(128)S(1)}, u32[32]{0:T(128)}, u32[]{:S(2)}) copy-start(u32[32]{0:T(128)} %constant.84) | copy-start | bytes 388
  36.6 436.8 %all-gather.4.cloned.1.call-start = ((), (), s32[]{:S(2)}) async-start(), calls=%async_computation.2 | async-start | bytes 23592960 | tf_op jit(solution)/shard_map/all_gather | solution.py:26
  495.8 2.1 copy-start.1
  498.0 11.1 %collective-permute-start = (f32[512,256]{1,0:T(8,128)S(1)}, f32[512,256]{1,0:T(8,128)S(1)}, u32[]{:S(2)}, u32[]{:S(2)}) collective-permute-start(f32[512,256]{1,0:T(8,128)S(1)} %slice_divide_fusion.1), channel_id=1, source_target_pairs={{0,1},{1,2},{2,3},{3,0},{4,5},{5,6},{6,7},{7,4},{8,9},{9,10},{10,1... | collective-permute-start | bytes 1572872 | tf_op jit(solution)/shard_map/ppermute | solution.py:17
  499.7 30.4 %collective-permute-start.2 = (f32[512,256]{1,0:T(8,128)S(1)}, f32[512,256]{1,0:T(8,128)S(1)}, u32[]{:S(2)}, u32[]{:S(2)}) collective-permute-start(f32[512,256]{1,0:T(8,128)S(1)} %slice_divide_fusion.1), channel_id=1, source_target_pairs={{0,3},{1,0},{2,1},{3,2},{4,7},{5,4},{6,5},{7,6},{8,11},{9,8},{10,9... | collective-permute-start | bytes 1572872 | tf_op jit(solution)/shard_map/ppermute | solution.py:19
  509.1 21.1 %collective-permute-start.1 = (f32[512,256]{1,0:T(8,128)S(1)}, f32[512,256]{1,0:T(8,128)}, u32[]{:S(2)}, u32[]{:S(2)}) collective-permute-start(f32[512,256]{1,0:T(8,128)S(1)} %collective-permute-done), channel_id=1, source_target_pairs={{0,1},{1,2},{2,3},{3,0},{4,5},{5,6},{6,7},{7,4},{8,9},{9,10},{10,1... | collective-permute-start | bytes 1572872 | tf_op jit(solution)/shard_map/ppermute | solution.py:17
  551.5 12.9 %collective-permute-start.3 = (f32[512,256]{1,0:T(8,128)S(1)}, f32[512,256]{1,0:T(8,128)S(1)}, u32[]{:S(2)}, u32[]{:S(2)}) collective-permute-start(f32[512,256]{1,0:T(8,128)S(1)} %multiply_subtract_fusion.1), channel_id=1, source_target_pairs={{0,1},{1,2},{2,3},{3,0},{4,5},{5,6},{6,7},{7,4},{8,9},{9,10},{10,1... | collective-permute-start | bytes 1572872 | tf_op jit(solution)/shard_map/ppermute | solution.py:17
  552.0 25.5 %collective-permute-start.5 = (f32[512,256]{1,0:T(8,128)S(1)}, f32[512,256]{1,0:T(8,128)S(1)}, u32[]{:S(2)}, u32[]{:S(2)}) collective-permute-start(f32[512,256]{1,0:T(8,128)S(1)} %multiply_subtract_fusion.1), channel_id=1, source_target_pairs={{0,3},{1,0},{2,1},{3,2},{4,7},{5,4},{6,5},{7,6},{8,11},{9,8},{10,9... | collective-permute-start | bytes 1572872 | tf_op jit(solution)/shard_map/ppermute | solution.py:19
  564.4 22.4 %collective-permute-start.4 = (f32[512,256]{1,0:T(8,128)S(1)}, f32[512,256]{1,0:T(8,128)S(1)}, u32[]{:S(2)}, u32[]{:S(2)}) collective-permute-start(f32[512,256]{1,0:T(8,128)S(1)} %collective-permute-done.3), channel_id=1, source_target_pairs={{0,1},{1,2},{2,3},{3,0},{4,5},{5,6},{6,7},{7,4},{8,9},{9,10},{10,1... | collective-permute-start | bytes 1572872 | tf_op jit(solution)/shard_map/ppermute | solution.py:17
  606.9 16.3 %collective-permute-start.6 = (f32[512,256]{1,0:T(8,128)S(1)}, f32[512,256]{1,0:T(8,128)S(1)}, u32[]{:S(2)}, u32[]{:S(2)}) collective-permute-start(f32[512,256]{1,0:T(8,128)S(1)} %get-tuple-element.65), channel_id=1, source_target_pairs={{0,1},{1,2},{2,3},{3,0},{4,5},{5,6},{6,7},{7,4},{8,9},{9,10},{10,1... | collective-permute-start | bytes 1572872 | tf_op jit(solution)/shard_map/ppermute | solution.py:17
  608.2 25.6 %collective-permute-start.8 = (f32[512,256]{1,0:T(8,128)S(1)}, f32[512,256]{1,0:T(8,128)S(1)}, u32[]{:S(2)}, u32[]{:S(2)}) collective-permute-start(f32[512,256]{1,0:T(8,128)S(1)} %get-tuple-element.65), channel_id=1, source_target_pairs={{0,3},{1,0},{2,1},{3,2},{4,7},{5,4},{6,5},{7,6},{8,11},{9,8},{10,9... | collective-permute-start | bytes 1572872 | tf_op jit(solution)/shard_map/ppermute | solution.py:19
  623.2 22.5 %collective-permute-start.7 = (f32[512,256]{1,0:T(8,128)S(1)}, f32[512,256]{1,0:T(8,128)}, u32[]{:S(2)}, u32[]{:S(2)}) collective-permute-start(f32[512,256]{1,0:T(8,128)S(1)} %collective-permute-done.6), channel_id=1, source_target_pairs={{0,1},{1,2},{2,3},{3,0},{4,5},{5,6},{6,7},{7,4},{8,9},{9,10},{10,1... | collective-permute-start | bytes 1572872 | tf_op jit(solution)/shard_map/ppermute | solution.py:17
Sparse Core Ops, SparseCore 0:
  36.7 315.1 reduce-scatter.1
  353.4 119.8 all-gather.3
